TPU v7x, 32 devices: a whole 2x2x4 slice. The times are simulated.
32 devices in a mesh: groups: 2 (over x), wide: 16 (over z, y, core).
Axes of the slice: x: 2, y: 2, z: 4, core: 2. Of those that a mesh axis runs over, the one named last changes fastest.
Arguments:
- prefix_hidden: bfloat16 [32, 256, 8192], P(('groups', 'wide')), parts along dimension 0, may hold values from -6 to 6
- prefix_lengths: int32 [32], P(('groups', 'wide')), parts along dimension 0, may hold values from 64 to 256
- action_noise: float32 [32, 50, 32], P(('groups', 'wide')), parts along dimension 0, may hold values from -4 to 4
- prefix_gain: float32 [8192], replicated, may hold values from 0.1 to 1.9
- key_weight: bfloat16 [8192, 512], P('wide'), may hold values from -0.0625 to 0.0625
- value_weight: bfloat16 [8192, 512], P('wide'), may hold values from -0.0625 to 0.0625
- input_weight: float32 [32, 1024], replicated, may hold values from -1 to 1
- expert_gain: float32 [1024], replicated, may hold values from 0.1 to 1.9
- expert_query: bfloat16 [1024, 1024], P('wide'), may hold values from -0.1875 to 0.1875
- expert_key: bfloat16 [1024, 512], P('wide'), may hold values from -5.3125 to 5.3125
- expert_value: bfloat16 [1024, 512], P('wide'), may hold values from -0.1875 to 0.1875
- expert_output: bfloat16 [1024, 1024], P('wide'), may hold values from -0.1875 to 0.1875
- final_gain: float32 [1024], replicated, may hold values from 0.1 to 1.9
- output_weight: bfloat16 [1024, 32], replicated, may hold values from -0.1875 to 0.1875
Outputs:
- actions: float32 [32, 50, 32], P(('groups', 'wide')), parts along dimension 0
There are 2 independent parts, one for each index of `groups`. A program takes and returns all parts, laid end to end along the dimension named above; an argument that names none is the same for every part. Nothing has to cross between parts.
Inputs may be any that keep to these rules, and one draw needn't show every extreme that they name: `prefix_lengths`: positions at or after a sample's length are padding and take no part.
All inputs are finite; a program needn't handle non-finite values.
Results may differ from a plain program's by a relative error of at most 0.0075.
Values may be sent and summed in bfloat16 or wider, within the bound.
A program may use at most 128 MiB of HBM per device.

v0:
```python
import jax
import jax.numpy as jnp
from jax import lax
from jax.sharding import PartitionSpec as P

HEAD = 128
STEPS = 4
rope_base = 1000000.0
norm_eps = 1e-06


def normalize(values, norm_gain):
    mean_square = jnp.mean(values * values, axis=-1, keepdims=True)
    return values * lax.rsqrt(mean_square + norm_eps) * norm_gain


def rotate(values, positions):
    half_width = values.shape[-1] // 2
    inv_freqs = rope_base ** (-jnp.arange(half_width, dtype=jnp.float32) * 2.0 / values.shape[-1])
    angles = positions[:, None] * inv_freqs[None, :]
    cosine = jnp.cos(angles)[:, None, :]
    sine_part = jnp.sin(angles)[:, None, :]
    first_half = values[..., :half_width]
    second = values[..., half_width:]
    return jnp.concatenate(
        [first_half * cosine - second * sine_part, second * cosine + first_half * sine_part], -1
    )


def time_embedding(time_value, embed_width):
    half_width = embed_width // 2
    fraction = jnp.arange(half_width, dtype=jnp.float32) / (half_width - 1)
    period = 0.004 * (4.0 / 0.004) ** fraction
    angles = time_value * (2.0 * jnp.pi) / period
    return jnp.concatenate([jnp.sin(angles), jnp.cos(angles)])


def attend(queries, key_cache, value_cache, action_keys, action_values, is_valid):
    span_rows = queries.shape[0]
    groups = key_cache.shape[1] // HEAD
    group_ratio = queries.shape[1] // key_cache.shape[1]
    query_heads = queries.reshape(span_rows, groups, group_ratio, HEAD)
    prefix_keys = key_cache.reshape(-1, groups, HEAD)
    prefix_values = value_cache.reshape(-1, groups, HEAD)
    own_keys = action_keys.reshape(span_rows, groups, HEAD)
    own_values = action_values.reshape(span_rows, groups, HEAD)
    prefix_scores = jnp.einsum(
        "cgrh,pgh->grcp", query_heads, prefix_keys, preferred_element_type=jnp.float32
    )
    prefix_scores = jnp.where(is_valid[None, None, None, :], prefix_scores, -1e30)
    own_scores = jnp.einsum(
        "cgrh,ngh->grcn", query_heads, own_keys, preferred_element_type=jnp.float32
    )
    row_max = jnp.maximum(jnp.max(prefix_scores, -1), jnp.max(own_scores, -1))[..., None]
    prefix_exp = jnp.exp(prefix_scores - row_max)
    own_exp = jnp.exp(own_scores - row_max)
    prob_total = jnp.sum(prefix_exp, -1, keepdims=True) + jnp.sum(own_exp, -1, keepdims=True)
    prefix_prob = (prefix_exp / prob_total).astype(jnp.bfloat16)
    own_prob = (own_exp / prob_total).astype(jnp.bfloat16)
    attn_mixed = jnp.einsum(
        "grcp,pgh->cgrh", prefix_prob, prefix_values, preferred_element_type=jnp.float32
    )
    attn_mixed = attn_mixed + jnp.einsum(
        "grcn,ngh->cgrh", own_prob, own_values, preferred_element_type=jnp.float32
    )
    return attn_mixed.reshape(span_rows, -1).astype(jnp.bfloat16)


def expert_steps(
    noise_rows,
    length,
    input_weight,
    expert_gain,
    query_w,
    key_w,
    value_w,
    output_w,
    final_gain,
    output_weight,
    key_cache,
    value_cache,
):
    span_rows = noise_rows.shape[0]
    is_valid = jnp.arange(key_cache.shape[0], dtype=jnp.int32) < length
    positions = length.astype(jnp.float32) + jnp.arange(span_rows, dtype=jnp.float32)
    action_state = noise_rows
    for step_idx in range(STEPS):
        time_value = 1.0 - step_idx / STEPS
        hidden = jnp.dot(
            action_state,
            input_weight,
            precision=lax.Precision.HIGHEST,
            preferred_element_type=jnp.float32,
        )
        hidden = hidden + time_embedding(time_value, input_weight.shape[1])[None, :]
        normed = normalize(hidden, expert_gain).astype(jnp.bfloat16)
        raw_queries = jnp.dot(normed, query_w, preferred_element_type=jnp.float32)
        queries = rotate(raw_queries.reshape(span_rows, -1, HEAD), positions).reshape(span_rows, -1)
        queries = (queries * HEAD ** (-0.5)).astype(jnp.bfloat16)
        raw_keys = jnp.dot(normed, key_w, preferred_element_type=jnp.float32)
        action_keys = (
            rotate(raw_keys.reshape(span_rows, -1, HEAD), positions)
            .reshape(span_rows, -1)
            .astype(jnp.bfloat16)
        )
        action_values = jnp.dot(normed, value_w, preferred_element_type=jnp.float32).astype(
            jnp.bfloat16
        )
        attn_mixed = attend(queries, key_cache, value_cache, action_keys, action_values, is_valid)
        hidden = hidden + jnp.dot(attn_mixed, output_w, preferred_element_type=jnp.float32)
        final_normed = normalize(hidden, final_gain).astype(jnp.bfloat16)
        velocity = jnp.dot(final_normed, output_weight, preferred_element_type=jnp.float32)
        action_state = action_state - velocity / STEPS
    return action_state


def shards(
    prefix_hidden,
    prefix_lengths,
    action_noise,
    prefix_gain,
    key_weight,
    value_weight,
    input_weight,
    expert_gain,
    expert_query,
    expert_key,
    expert_value,
    expert_output,
    final_gain,
    output_weight,
):
    gathered = (
        lax.all_gather(expert_query, "wide", axis=0, tiled=True),
        lax.all_gather(expert_key, "wide", axis=0, tiled=True),
        lax.all_gather(expert_value, "wide", axis=0, tiled=True),
        lax.all_gather(expert_output, "wide", axis=0, tiled=True),
    )
    hidden = prefix_hidden[0]
    row_count = hidden.shape[0]
    normed = normalize(hidden.astype(jnp.float32), prefix_gain).astype(jnp.bfloat16)
    stacked = jnp.stack([key_weight, value_weight], 0)
    projected = jnp.einsum(
        "pd,kdc->pkc",
        normed,
        lax.all_gather(stacked, "wide", axis=1, tiled=True),
        preferred_element_type=jnp.float32,
    )
    positions = jnp.arange(row_count, dtype=jnp.float32)
    key_cache = (
        rotate(projected[:, 0].reshape(row_count, -1, HEAD), positions)
        .reshape(row_count, -1)
        .astype(jnp.bfloat16)
    )
    value_cache = projected[:, 1].astype(jnp.bfloat16)
    query_w, key_w, value_w, output_w = gathered
    action_state = expert_steps(
        action_noise[0],
        prefix_lengths[0],
        input_weight,
        expert_gain,
        query_w,
        key_w,
        value_w,
        output_w,
        final_gain,
        output_weight,
        key_cache,
        value_cache,
    )
    return action_state[None]


def solution(mesh):
    placed = (
        P(("groups", "wide"), None, None),
        P(("groups", "wide")),
        P(("groups", "wide"), None, None),
        P(),
        P("wide", None),
        P("wide", None),
        P(),
        P(),
        P("wide", None),
        P("wide", None),
        P("wide", None),
        P("wide", None),
        P(),
        P(),
    )
    return jax.shard_map(
        shards,
        mesh=mesh,
        in_specs=placed,
        out_specs=P(("groups", "wide"), None, None),
        check_vma=False,
    )
```

profile of v0, /device:TPU:0, one launch (start us, length us, event | category | flops | bytes accessed | tf_op | source)
XLA Modules:
  0.0 368.0 jit_solution(7898720133912089493)
XLA Ops:
  6.5 0.7 all-gather.10.cloned.1.call-update
  7.3 0.7 all-gather.12.cloned.1.call-update
  8.1 0.7 all-gather.8.cloned.1.call-update
  8.8 2.3 pad_maximum_fusion
  11.1 0.5 all-gather.14.cloned.1.call-update
  12.0 3.1 fusion
  15.1 0.5 fusion.47
  17.1 0.6 pad_maximum_fusion.2
  17.7 0.6 pad_maximum_fusion.3
  18.3 0.6 pad_maximum_fusion.4
  19.0 31.2 %all-gather.10.cloned.1.call-done = bf16[1024,512]{1,0:T(8,128)(2,1)} async-done(((bf16[64,512]{1,0:T(8,128)(2,1)}), bf16[1024,512]{1,0:T(8,128)(2,1)}) %all-gather.10.cloned.1.call-update) | async-done | bytes 1048592 | tf_op jit(solution)/shard_map/all_gather | solution.py:135
  50.2 1.5 fusion.107
  51.9 37.4 %all-gather.12.cloned.1.call-done = bf16[1024,512]{1,0:T(8,128)(2,1)} async-done(((bf16[64,512]{1,0:T(8,128)(2,1)}), bf16[1024,512]{1,0:T(8,128)(2,1)}) %all-gather.12.cloned.1.call-update) | async-done | bytes 1048592 | tf_op jit(solution)/shard_map/all_gather | solution.py:136
  89.2 1.5 convolution_convert_fusion.3
  90.7 0.6 reshape.309
  91.4 40.4 %all-gather.8.cloned.1.call-done = bf16[1024,1024]{1,0:T(8,128)(2,1)} async-done(((bf16[64,1024]{1,0:T(8,128)(2,1)}), bf16[1024,1024]{1,0:T(8,128)(2,1)}) %all-gather.8.cloned.1.call-update) | async-done | bytes 2097168 | tf_op jit(solution)/shard_map/all_gather | solution.py:134
  131.9 2.1 fusion.106
  134.6 124.5 %all-gather.6.cloned.1.call-done = bf16[2,8192,512]{2,1,0:T(8,128)(2,1)} async-done(((bf16[2,512,512]{2,1,0:T(8,128)(2,1)}), bf16[2,8192,512]{2,1,0:T(8,128)(2,1)}) %all-gather.6.cloned.1.call-update) | async-done | bytes 16777232 | tf_op jit(solution)/shard_map/all_gather | solution.py:146
  259.1 9.5 %fusion.4 = f32[256,2,512]{2,0,1:T(8,128)S(1)} fusion(bf16[2,8192,512]{2,1,0:T(8,128)(2,1)} %all-gather.6.cloned.1.call-done, bf16[1,256,8192]{2,1,0:T(8,128)(2,1)} %param.14, f32[8192]{0:T(1024)S(1)} %copy-done.58, f32[256]{0:T(256)S(1)} %add_rsqrt_fusion), kind=kOutput, calls=%fused_computation.6 | convolution fusion | flops 4303355904 | bytes 22053888 | tf_op jit(solution)/shard_map/pd,kdc->pkc/dot_general | solution.py:143
  271.2 29.5 %all-gather.14.cloned.1.call-done = bf16[1024,1024]{1,0:T(8,128)(2,1)} async-done(((bf16[64,1024]{1,0:T(8,128)(2,1)}), bf16[1024,1024]{1,0:T(8,128)(2,1)}) %all-gather.14.cloned.1.call-update) | async-done | bytes 2097168 | tf_op jit(solution)/shard_map/all_gather | solution.py:137
  300.8 2.2 multiply_reduce_fusion.6
  303.9 0.6 copy-done.21
  305.3 0.6 copy-done.34
  306.0 1.7 fusion.100
  307.7 0.9 fusion.109
  308.6 1.6 reshape.311
  310.2 1.1 fusion.96
  311.3 0.8 subtract_convert_fusion.3
  312.1 1.2 fusion.101
  313.3 0.7 max.29
  314.1 1.3 fusion.27
  315.5 2.1 fusion.31
  317.6 0.9 convolution_convert_fusion.2
  318.5 1.5 reshape.312
  320.0 1.3 fusion.19
  321.3 0.7 copy.50
  322.0 1.6 convert_element_type.174
  323.6 2.2 multiply_reduce_fusion.4
  326.7 0.7 copy-done.22
  328.4 0.6 copy-done.35
  329.0 1.1 fusion.102
  330.1 0.9 fusion.111
  331.1 1.6 reshape.314
  332.6 1.1 fusion.95
  333.7 0.8 subtract_convert_fusion.2
  334.5 1.2 fusion.103
  335.7 1.4 fusion.28
  337.2 2.1 fusion.32
  339.3 0.9 convolution_convert_fusion.1
  340.2 1.5 reshape.315
  341.7 1.3 fusion.18
  343.0 0.7 copy.57
  343.7 1.6 convert_element_type.184
  345.3 2.2 multiply_reduce_fusion.2
  347.6 1.0 fusion.23
  348.6 1.2 multiply_reduce_fusion.1
  349.8 0.7 copy-done.19
  350.5 0.8 multiply_convert_fusion.1
  354.5 2.3 fusion.33
  356.7 0.9 convolution_convert_fusion
  357.7 0.9 reshape.318
  358.5 1.3 fusion.17
  360.0 0.6 multiply_reduce_fusion
  360.6 0.8 fusion.22
  (205 shorter events, 11.1 us)
Async XLA Ops:
  6.5 9.1 %copy-start = (f32[32,1024]{1,0:T(8,128)S(1)}, f32[32,1024]{1,0:T(8,128)}, u32[]{:S(2)}) copy-start(f32[32,1024]{1,0:T(8,128)} %param.20) | copy-start | bytes 393220
  6.5 43.7 %all-gather.10.cloned.1.call-start = ((), (), s32[]{:S(2)}) async-start(), calls=%async_computation.2 | async-start | bytes 1114112 | tf_op jit(solution)/shard_map/all_gather | solution.py:135
  7.3 82.0 %all-gather.12.cloned.1.call-start = ((), (), s32[]{:S(2)}) async-start(), calls=%async_computation.3 | async-start | bytes 1114112 | tf_op jit(solution)/shard_map/all_gather | solution.py:136
  8.0 123.8 %all-gather.8.cloned.1.call-start = ((), (), s32[]{:S(2)}) async-start(), calls=%async_computation.1 | async-start | bytes 2228224 | tf_op jit(solution)/shard_map/all_gather | solution.py:134
  8.7 250.4 %all-gather.6.cloned.1.call-start = ((), (), s32[]{:S(2)}) async-start(), calls=%async_computation | async-start | bytes 17825792 | tf_op jit(solution)/shard_map/all_gather | solution.py:146
  11.1 289.7 %all-gather.14.cloned.1.call-start = ((), (), s32[]{:S(2)}) async-start(), calls=%async_computation.4 | async-start | bytes 2228224 | tf_op jit(solution)/shard_map/all_gather | solution.py:137
  11.9 3.7 %copy-start.44 = (f32[1,50,32]{1,2,0:T(8,128)S(1)}, f32[1,50,32]{1,2,0:T(8,128)}, u32[]{:S(2)}) copy-start(f32[1,50,32]{1,2,0:T(8,128)} %param.16) | copy-start | bytes 19204
  12.0 6.9 %copy-start.41 = (f32[1024]{0:T(1024)S(1)}, f32[1024]{0:T(1024)}, u32[]{:S(2)}) copy-start(f32[1024]{0:T(1024)} %param.21) | copy-start | bytes 12292
  16.1 117.8 %copy-start.17 = (f32[50,1024]{1,0:T(8,128)}, f32[50,1024]{1,0:T(8,128)S(1)}, u32[]{:S(2)}) copy-start(f32[50,1024]{1,0:T(8,128)S(1)} %get-tuple-element.38) | copy-start | bytes 614404
  17.0 117.0 %copy-start.7 = (f32[50,64]{1,0:T(8,128)}, f32[50,64]{1,0:T(8,128)S(1)}, u32[]{:S(2)}) copy-start(f32[50,64]{1,0:T(8,128)S(1)} %get-tuple-element.33) | copy-start | bytes 38404
  17.0 117.0 %copy-start.12 = (f32[50,64]{1,0:T(8,128)}, f32[50,64]{1,0:T(8,128)S(1)}, u32[]{:S(2)}) copy-start(f32[50,64]{1,0:T(8,128)S(1)} %get-tuple-element.34) | copy-start | bytes 38404
  17.0 252.6 %copy-start.53 = (pred[256]{0:T(512)(128)(4,1)}, pred[256]{0:T(512)(128)(4,1)S(1)}, u32[]{:S(2)}) copy-start(pred[256]{0:T(512)(128)(4,1)S(1)} %iota_compare_fusion) | copy-start | bytes 772
  91.4 167.7 %copy-start.58 = (f32[8192]{0:T(1024)S(1)}, f32[8192]{0:T(1024)}, u32[]{:S(2)}) copy-start(f32[8192]{0:T(1024)} %param.17) | copy-start | bytes 98308
  269.0 1.4 copy-start.39
  269.7 1.1 copy-start.49
  270.1 30.6 %copy-start.18 = (f32[50,1024]{1,0:T(8,128)S(1)}, f32[50,1024]{1,0:T(8,128)}, u32[]{:S(2)}) copy-start(f32[50,1024]{1,0:T(8,128)} %copy-done.17) | copy-start | bytes 614404
  270.8 32.2 %copy-start.30 = (bf16[1024,32]{0,1:T(8,128)(2,1)S(1)}, bf16[1024,32]{0,1:T(8,128)(2,1)}, u32[]{:S(2)}) copy-start(bf16[1024,32]{0,1:T(8,128)(2,1)} %param.27) | copy-start | bytes 196612
  270.8 32.2 %copy-start.45 = (f32[1,50,32]{1,2,0:T(8,128)S(1)}, f32[1,50,32]{1,2,0:T(8,128)}, u32[]{:S(2)}) copy-start(f32[1,50,32]{1,2,0:T(8,128)} %param.16) | copy-start | bytes 19204
  270.8 32.2 %copy-start.46 = (f32[1024]{0:T(1024)S(1)}, f32[1024]{0:T(1024)}, u32[]{:S(2)}) copy-start(f32[1024]{0:T(1024)} %param.26) | copy-start | bytes 12292
  270.8 32.4 %copy-start.52 = (f32[1024]{0:T(1024)S(1)}, f32[1024]{0:T(1024)}, u32[]{:S(2)}) copy-start(f32[1024]{0:T(1024)} %pad_maximum_fusion.2) | copy-start | bytes 12292
  271.1 32.7 %copy-start.42 = (f32[1024]{0:T(1024)S(1)}, f32[1024]{0:T(1024)}, u32[]{:S(2)}) copy-start(f32[1024]{0:T(1024)} %param.21) | copy-start | bytes 12292
  271.1 33.4 %copy-start.1 = (bf16[1024,1024]{1,0:T(8,128)(2,1)S(1)}, bf16[1024,1024]{1,0:T(8,128)(2,1)}, u32[]{:S(2)}) copy-start(bf16[1024,1024]{1,0:T(8,128)(2,1)} %all-gather.8.cloned.1.call-done) | copy-start | bytes 6291460
  303.2 1.8 copy-start.8
  303.2 1.8 copy-start.13
  303.7 0.7 copy-start.21
  304.4 3.2 copy-start.25
  304.4 1.5 copy-start.54
  304.9 2.7 copy-start.4
  305.3 0.7 copy-start.34
  310.2 7.4 %copy-start.3 = (bf16[1024,512]{1,0:T(8,128)(2,1)S(1)}, bf16[1024,512]{1,0:T(8,128)(2,1)}, u32[]{:S(2)}) copy-start(bf16[1024,512]{1,0:T(8,128)(2,1)} %all-gather.12.cloned.1.call-done) | copy-start | bytes 3145732
  310.2 7.4 %copy-start.26 = (bf16[50,1024]{1,0:T(8,128)(2,1)S(1)}, bf16[50,1024]{1,0:T(8,128)(2,1)}, u32[]{:S(2)}) copy-start(bf16[50,1024]{1,0:T(8,128)(2,1)} %copy-done.25) | copy-start | bytes 307204
  313.3 2.0 copy-start.37
  314.1 1.4 copy-start.50
  315.4 2.1 copy-start.57
  323.6 2.3 copy-start.31
  323.6 2.3 copy-start.47
  323.6 2.5 copy-start.51
  323.6 3.7 %copy-start.43 = (f32[1024]{0:T(1024)S(1)}, f32[1024]{0:T(1024)}, u32[]{:S(2)}) copy-start(f32[1024]{0:T(1024)} %param.21) | copy-start | bytes 12292
  326.1 1.9 copy-start.40
  326.2 1.9 copy-start.9
  326.2 1.9 copy-start.14
  326.7 0.7 copy-start.22
  327.4 2.7 copy-start.27
  327.5 1.6 copy-start.55
  327.9 2.2 copy-start.5
  328.4 0.7 copy-start.35
  332.6 6.7 %copy-start.28 = (bf16[50,1024]{1,0:T(8,128)(2,1)S(1)}, bf16[50,1024]{1,0:T(8,128)(2,1)}, u32[]{:S(2)}) copy-start(bf16[50,1024]{1,0:T(8,128)(2,1)} %copy-done.27) | copy-start | bytes 307204
  335.7 1.4 copy-start.38
  345.3 2.2 copy-start.32
  348.5 3.3 copy-start.10
  348.5 3.3 copy-start.15
  349.7 0.7 copy-start.19
  351.2 1.3 copy-start.23
  351.2 0.9 copy-start.56
  351.7 1.2 copy-start.6
  351.8 1.6 copy-start.11
  351.9 1.6 copy-start.16
  353.0 1.2 copy-start.29
  353.3 3.4 copy-start.24
  353.8 0.7 copy-start.36
  354.5 5.5 %copy-start.2 = (bf16[1024,1024]{1,0:T(8,128)(2,1)S(1)}, bf16[1024,1024]{1,0:T(8,128)(2,1)}, u32[]{:S(2)}) copy-start(bf16[1024,1024]{1,0:T(8,128)(2,1)} %all-gather.14.cloned.1.call-done) | copy-start | bytes 6291460
  354.5 5.5 %copy-start.20 = (f32[50,1024]{1,0:T(8,128)S(1)}, f32[50,1024]{1,0:T(8,128)}, u32[]{:S(2)}) copy-start(f32[50,1024]{1,0:T(8,128)} %copy-done.19) | copy-start | bytes 614404
  357.6 2.9 copy-start.33
  357.6 2.9 copy-start.48
Sparse Core Ops, SparseCore 0:
  9.5 40.6 all-gather.9
  52.4 36.8 all-gather.11
  91.4 40.4 all-gather.7
  133.9 125.1 all-gather.5
  261.1 39.6 all-gather.13
where the time goes:
time: 369 us; the launch traced here: 368 us
  waiting for transfers between devices  266 us (72%)
  matrix products  50.5 us (14%)
  local copies, waits for them, and re-layouts  20.1 us (5%)
  other arithmetic  16.4 us (4%)
  between operations  15.1 us (4%)
    all_gather x1, waiting for transfers between devices, shards(): lax.all_gather(stacked, 'wide', axis=1, tiled=True)  124 us
    all_gather x1, waiting for transfers between devices, shards(): lax.all_gather(expert_query, 'wide', axis=0, tiled=True)  40.4 us
    all_gather x1, waiting for transfers between devices, shards(): lax.all_gather(expert_value, 'wide', axis=0, tiled=True)  37.4 us
    all_gather x1, waiting for transfers between devices, shards(): lax.all_gather(expert_key, 'wide', axis=0, tiled=True)  31.2 us
    all_gather x1, waiting for transfers between devices, shards(): lax.all_gather(expert_output, 'wide', axis=0, tiled=True)  29.5 us
    dot_general x1, matrix products, shards(): jnp.einsum('pd,kdc->pkc', normed, lax.all_gather(stacked, 'wide', axis=1,...  9.54 us
  transfers between devices with their start and end apart: 5, of which 5 were waited for; matrix products, arithmetic and copies ran while one was open for 7% of the time, Pallas kernels for 0%

commit v1 on v0

--- a/solution.py
+++ b/solution.py
@@ -7,6 +7,23 @@
 STEPS = 4
 rope_base = 1000000.0
 norm_eps = 1e-06
+
+
+def laid_out(blocks, dim):
+    dims = list(blocks.shape[1:])
+    dims[dim] *= blocks.shape[0]
+    return jnp.moveaxis(blocks, 0, dim).reshape(dims)
+
+
+def collect(value, axis, dim):
+    peers = lax.axis_size(axis)
+    forward = [(i, (i + 1) % peers) for i in range(peers)]
+    blocks = [value]
+    while len(blocks) < peers:
+        blocks.append(lax.ppermute(blocks[-1], axis, forward))
+    place = lax.axis_index(axis)
+    blocks = jnp.stack(blocks)[(place - jnp.arange(peers)) % peers]
+    return laid_out(blocks, dim)
 
 
 def normalize(values, norm_gain):
@@ -133,7 +150,7 @@
     gathered = (
         lax.all_gather(expert_query, "wide", axis=0, tiled=True),
         lax.all_gather(expert_key, "wide", axis=0, tiled=True),
-        lax.all_gather(expert_value, "wide", axis=0, tiled=True),
+        collect(expert_value, "wide", 0),
         lax.all_gather(expert_output, "wide", axis=0, tiled=True),
     )
     hidden = prefix_hidden[0]

time: 369 us -> 333 us (0.902)
  waiting for transfers between devices: 266 us -> 226 us
    ppermute x0 -> x15, waiting for transfers between devices: none -> 91.8 us  [collect(): blocks.append(lax.ppermute(blocks[-1], axis, forward))]
    all_gather x1, waiting for transfers between devices: 40.4 us -> 0.02 us  [shards(): lax.all_gather(expert_query, 'wide', axis=0, tiled=True)]
    all_gather x1 -> x0, waiting for transfers between devices: 37.4 us -> none  [shards(): lax.all_gather(expert_value, 'wide', axis=0, tiled=True)]
    all_gather x1, waiting for transfers between devices: 31.2 us -> 0.02 us  [shards(): lax.all_gather(expert_key, 'wide', axis=0, tiled=True)]
    all_gather x1, waiting for transfers between devices: 124 us -> 104 us  [shards(): lax.all_gather(stacked, 'wide', axis=1, tiled=True)]
  transfers between devices with their start and end apart: 5 -> 19, of which waited for: 5 -> 16; matrix products, arithmetic and copies ran while one was open for 7% -> 8% of each run, Pallas kernels for 0% -> 0%
where the time goes in v1:
time: 333 us; the launch traced here: 331 us
  waiting for transfers between devices  226 us (68%)
  matrix products  49.4 us (15%)
  local copies, waits for them, and re-layouts  20.2 us (6%)
  other arithmetic  17.1 us (5%)
  between operations  15.1 us (5%)
  starting transfers between devices  3.37 us (1%)
    all_gather x1, waiting for transfers between devices, shards(): lax.all_gather(stacked, 'wide', axis=1, tiled=True)  104 us
    ppermute x15, waiting for transfers between devices, collect(): blocks.append(lax.ppermute(blocks[-1], axis, forward))  91.8 us
    all_gather x1, waiting for transfers between devices, shards(): lax.all_gather(expert_output, 'wide', axis=0, tiled=True)  29 us
    dot_general x1, matrix products, shards(): jnp.einsum('pd,kdc->pkc', normed, lax.all_gather(stacked, 'wide', axis=1,...  9.59 us
    dot_general x4, matrix products, expert_steps(): jnp.dot(attn_mixed, output_w, preferred_element_type=jnp.float32)  7.24 us
  transfers between devices with their start and end apart: 19, of which 16 were waited for; matrix products, arithmetic and copies ran while one was open for 8% of the time, Pallas kernels for 0%

profile of v1, /device:TPU:0, one launch (start us, length us, event | category | flops | bytes accessed | tf_op | source)
XLA Modules:
  0.0 331.4 jit_solution(3031819663181391979)
XLA Ops:
  6.5 0.7 all-gather.9.cloned.1.call-update
  8.1 2.3 pad_maximum_fusion
  11.3 3.1 fusion
  18.4 2.7 collective-permute-start.1
  21.0 4.9 %collective-permute-done.1 = bf16[64,512]{1,0:T(8,128)(2,1)S(1)} collective-permute-done((bf16[64,512]{1,0:T(8,128)(2,1)S(1)}, bf16[64,512]{1,0:T(8,128)(2,1)S(1)}, u32[]{:S(2)}, u32[]{:S(2)}) %collective-permute-start.1) | collective-permute-done | bytes 65568 | tf_op jit(solution)/shard_map/ppermute | solution.py:23
  25.9 6.4 %collective-permute-done.2 = bf16[64,512]{1,0:T(8,128)(2,1)S(1)} collective-permute-done((bf16[64,512]{1,0:T(8,128)(2,1)S(1)}, bf16[64,512]{1,0:T(8,128)(2,1)S(1)}, u32[]{:S(2)}, u32[]{:S(2)}) %collective-permute-start.2) | collective-permute-done | bytes 65568 | tf_op jit(solution)/shard_map/ppermute | solution.py:23
  32.4 6.4 %collective-permute-done.3 = bf16[64,512]{1,0:T(8,128)(2,1)S(1)} collective-permute-done((bf16[64,512]{1,0:T(8,128)(2,1)S(1)}, bf16[64,512]{1,0:T(8,128)(2,1)S(1)}, u32[]{:S(2)}, u32[]{:S(2)}) %collective-permute-start.3) | collective-permute-done | bytes 65568 | tf_op jit(solution)/shard_map/ppermute | solution.py:23
  38.8 6.6 %collective-permute-done.4 = bf16[64,512]{1,0:T(8,128)(2,1)S(1)} collective-permute-done((bf16[64,512]{1,0:T(8,128)(2,1)S(1)}, bf16[64,512]{1,0:T(8,128)(2,1)S(1)}, u32[]{:S(2)}, u32[]{:S(2)}) %collective-permute-start.4) | collective-permute-done | bytes 65568 | tf_op jit(solution)/shard_map/ppermute | solution.py:23
  45.4 6.4 %collective-permute-done.5 = bf16[64,512]{1,0:T(8,128)(2,1)S(1)} collective-permute-done((bf16[64,512]{1,0:T(8,128)(2,1)S(1)}, bf16[64,512]{1,0:T(8,128)(2,1)S(1)}, u32[]{:S(2)}, u32[]{:S(2)}) %collective-permute-start.5) | collective-permute-done | bytes 65568 | tf_op jit(solution)/shard_map/ppermute | solution.py:23
  51.8 6.4 %collective-permute-done.6 = bf16[64,512]{1,0:T(8,128)(2,1)S(1)} collective-permute-done((bf16[64,512]{1,0:T(8,128)(2,1)S(1)}, bf16[64,512]{1,0:T(8,128)(2,1)S(1)}, u32[]{:S(2)}, u32[]{:S(2)}) %collective-permute-start.6) | collective-permute-done | bytes 65568 | tf_op jit(solution)/shard_map/ppermute | solution.py:23
  58.2 6.5 %collective-permute-done.7 = bf16[64,512]{1,0:T(8,128)(2,1)S(1)} collective-permute-done((bf16[64,512]{1,0:T(8,128)(2,1)S(1)}, bf16[64,512]{1,0:T(8,128)(2,1)S(1)}, u32[]{:S(2)}, u32[]{:S(2)}) %collective-permute-start.7) | collective-permute-done | bytes 65568 | tf_op jit(solution)/shard_map/ppermute | solution.py:23
  64.7 7.1 %collective-permute-done.8 = bf16[64,512]{1,0:T(8,128)(2,1)S(1)} collective-permute-done((bf16[64,512]{1,0:T(8,128)(2,1)S(1)}, bf16[64,512]{1,0:T(8,128)(2,1)S(1)}, u32[]{:S(2)}, u32[]{:S(2)}) %collective-permute-start.8) | collective-permute-done | bytes 65568 | tf_op jit(solution)/shard_map/ppermute | solution.py:23
  71.8 6.4 %collective-permute-done.9 = bf16[64,512]{1,0:T(8,128)(2,1)S(1)} collective-permute-done((bf16[64,512]{1,0:T(8,128)(2,1)S(1)}, bf16[64,512]{1,0:T(8,128)(2,1)S(1)}, u32[]{:S(2)}, u32[]{:S(2)}) %collective-permute-start.9) | collective-permute-done | bytes 65568 | tf_op jit(solution)/shard_map/ppermute | solution.py:23
  78.2 7.9 %collective-permute-done.10 = bf16[64,512]{1,0:T(8,128)(2,1)S(1)} collective-permute-done((bf16[64,512]{1,0:T(8,128)(2,1)S(1)}, bf16[64,512]{1,0:T(8,128)(2,1)S(1)}, u32[]{:S(2)}, u32[]{:S(2)}) %collective-permute-start.10) | collective-permute-done | bytes 65568 | tf_op jit(solution)/shard_map/ppermute | solution.py:23
  86.1 6.4 %collective-permute-done.11 = bf16[64,512]{1,0:T(8,128)(2,1)S(1)} collective-permute-done((bf16[64,512]{1,0:T(8,128)(2,1)S(1)}, bf16[64,512]{1,0:T(8,128)(2,1)S(1)}, u32[]{:S(2)}, u32[]{:S(2)}) %collective-permute-start.11) | collective-permute-done | bytes 65568 | tf_op jit(solution)/shard_map/ppermute | solution.py:23
  92.5 6.4 %collective-permute-done.12 = bf16[64,512]{1,0:T(8,128)(2,1)S(1)} collective-permute-done((bf16[64,512]{1,0:T(8,128)(2,1)S(1)}, bf16[64,512]{1,0:T(8,128)(2,1)S(1)}, u32[]{:S(2)}, u32[]{:S(2)}) %collective-permute-start.12) | collective-permute-done | bytes 65568 | tf_op jit(solution)/shard_map/ppermute | solution.py:23
  98.9 6.4 %collective-permute-done.13 = bf16[64,512]{1,0:T(8,128)(2,1)S(1)} collective-permute-done((bf16[64,512]{1,0:T(8,128)(2,1)S(1)}, bf16[64,512]{1,0:T(8,128)(2,1)S(1)}, u32[]{:S(2)}, u32[]{:S(2)}) %collective-permute-start.13) | collective-permute-done | bytes 65568 | tf_op jit(solution)/shard_map/ppermute | solution.py:23
  105.3 7.7 %collective-permute-done.14 = bf16[64,512]{1,0:T(8,128)(2,1)S(1)} collective-permute-done((bf16[64,512]{1,0:T(8,128)(2,1)S(1)}, bf16[64,512]{1,0:T(8,128)(2,1)S(1)}, u32[]{:S(2)}, u32[]{:S(2)}) %collective-permute-start.14) | collective-permute-done | bytes 65568 | tf_op jit(solution)/shard_map/ppermute | solution.py:23
  114.0 1.5 fusion.109
  115.8 2.1 fusion.108
  118.5 104.0 %all-gather.5.cloned.1.call-done = bf16[2,8192,512]{2,1,0:T(8,128)(2,1)} async-done(((bf16[2,512,512]{2,1,0:T(8,128)(2,1)}), bf16[2,8192,512]{2,1,0:T(8,128)(2,1)}) %all-gather.5.cloned.1.call-update) | async-done | bytes 16777232 | tf_op jit(solution)/shard_map/all_gather | solution.py:163
  222.5 9.6 %fusion.4 = f32[256,2,512]{2,0,1:T(8,128)S(1)} fusion(bf16[2,8192,512]{2,1,0:T(8,128)(2,1)} %all-gather.5.cloned.1.call-done, bf16[1,256,8192]{2,1,0:T(8,128)(2,1)} %param.14, f32[8192]{0:T(1024)S(1)} %copy-done.46, f32[256]{0:T(256)S(1)} %add_rsqrt_fusion), kind=kOutput, calls=%fused_computation.7 | convolution fusion | flops 4303355904 | bytes 22053888 | tf_op jit(solution)/shard_map/pd,kdc->pkc/dot_general | solution.py:160
  234.5 0.7 convert_element_type.164
  235.2 29.0 %all-gather.11.cloned.1.call-done = bf16[1024,1024]{1,0:T(8,128)(2,1)} async-done(((bf16[64,1024]{1,0:T(8,128)(2,1)}), bf16[1024,1024]{1,0:T(8,128)(2,1)}) %all-gather.11.cloned.1.call-update) | async-done | bytes 2097168 | tf_op jit(solution)/shard_map/all_gather | solution.py:154
  264.2 2.2 multiply_reduce_fusion.6
  266.4 1.0 fusion.25
  267.4 1.2 multiply_reduce_fusion.5
  269.3 0.8 multiply_convert_fusion.5
  270.1 0.9 convolution_convert_fusion.2
  272.5 1.7 fusion.102
  274.2 0.9 fusion.111
  275.1 1.6 reshape.364
  276.7 1.1 fusion.98
  277.8 0.8 subtract_convert_fusion.3
  278.6 1.2 fusion.103
  279.8 0.7 max.29
  280.5 1.3 fusion.27
  282.5 2.1 fusion.31
  284.6 1.5 reshape.365
  286.1 1.3 fusion.19
  287.4 0.7 copy.50
  288.1 1.6 convert_element_type.174
  289.7 2.2 multiply_reduce_fusion.4
  293.6 0.9 convolution_convert_fusion.1
  296.0 1.1 fusion.104
  297.1 0.9 fusion.113
  298.0 1.6 reshape.367
  299.6 1.1 fusion.97
  300.7 0.8 subtract_convert_fusion.2
  301.5 1.2 fusion.105
  302.7 1.4 fusion.28
  304.2 2.1 fusion.32
  306.3 1.5 reshape.368
  307.7 1.3 fusion.18
  309.0 0.7 copy.57
  309.8 1.6 convert_element_type.184
  311.3 2.2 multiply_reduce_fusion.2
  313.6 1.0 fusion.23
  314.6 1.2 multiply_reduce_fusion.1
  316.5 0.8 multiply_convert_fusion.1
  317.3 0.9 convolution_convert_fusion
  321.1 1.0 fusion.33
  322.1 1.2 fusion.17
  324.1 0.8 fusion.22
  (227 shorter events, 19.0 us)
Async XLA Ops:
  6.5 8.4 %copy-start = (f32[32,1024]{1,0:T(8,128)S(1)}, f32[32,1024]{1,0:T(8,128)}, u32[]{:S(2)}) copy-start(f32[32,1024]{1,0:T(8,128)} %param.20) | copy-start | bytes 393220
  6.5 3.9 %copy-start.35 = (bf16[64,512]{1,0:T(8,128)(2,1)S(1)}, bf16[64,512]{1,0:T(8,128)(2,1)}, u32[]{:S(2)}) copy-start(bf16[64,512]{1,0:T(8,128)(2,1)} %param.24) | copy-start | bytes 196612
  6.5 107.5 %all-gather.9.cloned.1.call-start = ((), (), s32[]{:S(2)}) async-start(), calls=%async_computation.2 | async-start | bytes 1114112 | tf_op jit(solution)/shard_map/all_gather | solution.py:152
  7.3 108.5 %all-gather.7.cloned.1.call-start = ((), (), s32[]{:S(2)}) async-start(), calls=%async_computation.1 | async-start | bytes 2228224 | tf_op jit(solution)/shard_map/all_gather | solution.py:151
  8.0 214.5 %all-gather.5.cloned.1.call-start = ((), (), s32[]{:S(2)}) async-start(), calls=%async_computation | async-start | bytes 17825792 | tf_op jit(solution)/shard_map/all_gather | solution.py:163
  10.4 253.8 %all-gather.11.cloned.1.call-start = ((), (), s32[]{:S(2)}) async-start(), calls=%async_computation.3 | async-start | bytes 2228224 | tf_op jit(solution)/shard_map/all_gather | solution.py:154
  10.4 7.9 %collective-permute-start = (bf16[64,512]{1,0:T(8,128)(2,1)S(1)}, bf16[64,512]{1,0:T(8,128)(2,1)S(1)}, u32[]{:S(2)}, u32[]{:S(2)}) collective-permute-start(bf16[64,512]{1,0:T(8,128)(2,1)S(1)} %copy-done.35), channel_id=1, source_target_pairs={{0,1},{1,2},{2,3},{3,4},{4,5},{5,6},{6,7},{7,8},{8,9},{9,10},{10,1... | collective-permute-start | bytes 196616 | tf_op jit(solution)/shard_map/ppermute | solution.py:23
  11.3 3.7 %copy-start.36 = (f32[1,50,32]{1,2,0:T(8,128)S(1)}, f32[1,50,32]{1,2,0:T(8,128)}, u32[]{:S(2)}) copy-start(f32[1,50,32]{1,2,0:T(8,128)} %param.16) | copy-start | bytes 19204
  11.3 6.9 %copy-start.33 = (f32[1024]{0:T(1024)S(1)}, f32[1024]{0:T(1024)}, u32[]{:S(2)}) copy-start(f32[1024]{0:T(1024)} %param.21) | copy-start | bytes 12292
  15.5 97.6 %copy-start.16 = (f32[50,1024]{1,0:T(8,128)}, f32[50,1024]{1,0:T(8,128)S(1)}, u32[]{:S(2)}) copy-start(f32[50,1024]{1,0:T(8,128)S(1)} %get-tuple-element.38) | copy-start | bytes 614404
  16.4 101.6 %copy-start.6 = (f32[50,64]{1,0:T(8,128)}, f32[50,64]{1,0:T(8,128)S(1)}, u32[]{:S(2)}) copy-start(f32[50,64]{1,0:T(8,128)S(1)} %get-tuple-element.33) | copy-start | bytes 38404
  16.4 101.6 %copy-start.11 = (f32[50,64]{1,0:T(8,128)}, f32[50,64]{1,0:T(8,128)S(1)}, u32[]{:S(2)}) copy-start(f32[50,64]{1,0:T(8,128)S(1)} %get-tuple-element.34) | copy-start | bytes 38404
  18.3 214.8 %copy-start.41 = (pred[256]{0:T(512)(128)(4,1)}, pred[256]{0:T(512)(128)(4,1)S(1)}, u32[]{:S(2)}) copy-start(pred[256]{0:T(512)(128)(4,1)S(1)} %iota_compare_fusion) | copy-start | bytes 772
  18.4 7.6 %collective-permute-start.1 = (bf16[64,512]{1,0:T(8,128)(2,1)S(1)}, bf16[64,512]{1,0:T(8,128)(2,1)S(1)}, u32[]{:S(2)}, u32[]{:S(2)}) collective-permute-start(bf16[64,512]{1,0:T(8,128)(2,1)S(1)} %collective-permute-done), channel_id=1, source_target_pairs={{0,1},{1,2},{2,3},{3,4},{4,5},{5,6},{6,7},{7,8},{8,9},{9,10},{10,1... | collective-permute-start | bytes 196616 | tf_op jit(solution)/shard_map/ppermute | solution.py:23
  25.9 6.4 %collective-permute-start.2 = (bf16[64,512]{1,0:T(8,128)(2,1)S(1)}, bf16[64,512]{1,0:T(8,128)(2,1)S(1)}, u32[]{:S(2)}, u32[]{:S(2)}) collective-permute-start(bf16[64,512]{1,0:T(8,128)(2,1)S(1)} %collective-permute-done.1), channel_id=1, source_target_pairs={{0,1},{1,2},{2,3},{3,4},{4,5},{5,6},{6,7},{7,8},{8,9},{9,10},{10,1... | collective-permute-start | bytes 196616 | tf_op jit(solution)/shard_map/ppermute | solution.py:23
  32.4 6.4 %collective-permute-start.3 = (bf16[64,512]{1,0:T(8,128)(2,1)S(1)}, bf16[64,512]{1,0:T(8,128)(2,1)S(1)}, u32[]{:S(2)}, u32[]{:S(2)}) collective-permute-start(bf16[64,512]{1,0:T(8,128)(2,1)S(1)} %collective-permute-done.2), channel_id=1, source_target_pairs={{0,1},{1,2},{2,3},{3,4},{4,5},{5,6},{6,7},{7,8},{8,9},{9,10},{10,1... | collective-permute-start | bytes 196616 | tf_op jit(solution)/shard_map/ppermute | solution.py:23
  38.8 6.6 %collective-permute-start.4 = (bf16[64,512]{1,0:T(8,128)(2,1)S(1)}, bf16[64,512]{1,0:T(8,128)(2,1)S(1)}, u32[]{:S(2)}, u32[]{:S(2)}) collective-permute-start(bf16[64,512]{1,0:T(8,128)(2,1)S(1)} %collective-permute-done.3), channel_id=1, source_target_pairs={{0,1},{1,2},{2,3},{3,4},{4,5},{5,6},{6,7},{7,8},{8,9},{9,10},{10,1... | collective-permute-start | bytes 196616 | tf_op jit(solution)/shard_map/ppermute | solution.py:23
  45.4 6.4 %collective-permute-start.5 = (bf16[64,512]{1,0:T(8,128)(2,1)S(1)}, bf16[64,512]{1,0:T(8,128)(2,1)S(1)}, u32[]{:S(2)}, u32[]{:S(2)}) collective-permute-start(bf16[64,512]{1,0:T(8,128)(2,1)S(1)} %collective-permute-done.4), channel_id=1, source_target_pairs={{0,1},{1,2},{2,3},{3,4},{4,5},{5,6},{6,7},{7,8},{8,9},{9,10},{10,1... | collective-permute-start | bytes 196616 | tf_op jit(solution)/shard_map/ppermute | solution.py:23
  51.8 6.4 %collective-permute-start.6 = (bf16[64,512]{1,0:T(8,128)(2,1)S(1)}, bf16[64,512]{1,0:T(8,128)(2,1)S(1)}, u32[]{:S(2)}, u32[]{:S(2)}) collective-permute-start(bf16[64,512]{1,0:T(8,128)(2,1)S(1)} %collective-permute-done.5), channel_id=1, source_target_pairs={{0,1},{1,2},{2,3},{3,4},{4,5},{5,6},{6,7},{7,8},{8,9},{9,10},{10,1... | collective-permute-start | bytes 196616 | tf_op jit(solution)/shard_map/ppermute | solution.py:23
  58.2 6.5 %collective-permute-start.7 = (bf16[64,512]{1,0:T(8,128)(2,1)S(1)}, bf16[64,512]{1,0:T(8,128)(2,1)S(1)}, u32[]{:S(2)}, u32[]{:S(2)}) collective-permute-start(bf16[64,512]{1,0:T(8,128)(2,1)S(1)} %collective-permute-done.6), channel_id=1, source_target_pairs={{0,1},{1,2},{2,3},{3,4},{4,5},{5,6},{6,7},{7,8},{8,9},{9,10},{10,1... | collective-permute-start | bytes 196616 | tf_op jit(solution)/shard_map/ppermute | solution.py:23
  64.7 7.1 %collective-permute-start.8 = (bf16[64,512]{1,0:T(8,128)(2,1)S(1)}, bf16[64,512]{1,0:T(8,128)(2,1)S(1)}, u32[]{:S(2)}, u32[]{:S(2)}) collective-permute-start(bf16[64,512]{1,0:T(8,128)(2,1)S(1)} %collective-permute-done.7), channel_id=1, source_target_pairs={{0,1},{1,2},{2,3},{3,4},{4,5},{5,6},{6,7},{7,8},{8,9},{9,10},{10,1... | collective-permute-start | bytes 196616 | tf_op jit(solution)/shard_map/ppermute | solution.py:23
  71.8 6.4 %collective-permute-start.9 = (bf16[64,512]{1,0:T(8,128)(2,1)S(1)}, bf16[64,512]{1,0:T(8,128)(2,1)S(1)}, u32[]{:S(2)}, u32[]{:S(2)}) collective-permute-start(bf16[64,512]{1,0:T(8,128)(2,1)S(1)} %collective-permute-done.8), channel_id=1, source_target_pairs={{0,1},{1,2},{2,3},{3,4},{4,5},{5,6},{6,7},{7,8},{8,9},{9,10},{10,1... | collective-permute-start | bytes 196616 | tf_op jit(solution)/shard_map/ppermute | solution.py:23
  78.2 7.9 %collective-permute-start.10 = (bf16[64,512]{1,0:T(8,128)(2,1)S(1)}, bf16[64,512]{1,0:T(8,128)(2,1)S(1)}, u32[]{:S(2)}, u32[]{:S(2)}) collective-permute-start(bf16[64,512]{1,0:T(8,128)(2,1)S(1)} %collective-permute-done.9), channel_id=1, source_target_pairs={{0,1},{1,2},{2,3},{3,4},{4,5},{5,6},{6,7},{7,8},{8,9},{9,10},{10,1... | collective-permute-start | bytes 196616 | tf_op jit(solution)/shard_map/ppermute | solution.py:23
  86.1 6.4 %collective-permute-start.11 = (bf16[64,512]{1,0:T(8,128)(2,1)S(1)}, bf16[64,512]{1,0:T(8,128)(2,1)S(1)}, u32[]{:S(2)}, u32[]{:S(2)}) collective-permute-start(bf16[64,512]{1,0:T(8,128)(2,1)S(1)} %collective-permute-done.10), channel_id=1, source_target_pairs={{0,1},{1,2},{2,3},{3,4},{4,5},{5,6},{6,7},{7,8},{8,9},{9,10},{10,1... | collective-permute-start | bytes 196616 | tf_op jit(solution)/shard_map/ppermute | solution.py:23
  92.5 6.4 %collective-permute-start.12 = (bf16[64,512]{1,0:T(8,128)(2,1)S(1)}, bf16[64,512]{1,0:T(8,128)(2,1)S(1)}, u32[]{:S(2)}, u32[]{:S(2)}) collective-permute-start(bf16[64,512]{1,0:T(8,128)(2,1)S(1)} %collective-permute-done.11), channel_id=1, source_target_pairs={{0,1},{1,2},{2,3},{3,4},{4,5},{5,6},{6,7},{7,8},{8,9},{9,10},{10,1... | collective-permute-start | bytes 196616 | tf_op jit(solution)/shard_map/ppermute | solution.py:23
  98.9 6.4 %collective-permute-start.13 = (bf16[64,512]{1,0:T(8,128)(2,1)S(1)}, bf16[64,512]{1,0:T(8,128)(2,1)S(1)}, u32[]{:S(2)}, u32[]{:S(2)}) collective-permute-start(bf16[64,512]{1,0:T(8,128)(2,1)S(1)} %collective-permute-done.12), channel_id=1, source_target_pairs={{0,1},{1,2},{2,3},{3,4},{4,5},{5,6},{6,7},{7,8},{8,9},{9,10},{10,1... | collective-permute-start | bytes 196616 | tf_op jit(solution)/shard_map/ppermute | solution.py:23
  105.3 7.7 %collective-permute-start.14 = (bf16[64,512]{1,0:T(8,128)(2,1)S(1)}, bf16[64,512]{1,0:T(8,128)(2,1)S(1)}, u32[]{:S(2)}, u32[]{:S(2)}) collective-permute-start(bf16[64,512]{1,0:T(8,128)(2,1)S(1)} %collective-permute-done.13), channel_id=1, source_target_pairs={{0,1},{1,2},{2,3},{3,4},{4,5},{5,6},{6,7},{7,8},{8,9},{9,10},{10,1... | collective-permute-start | bytes 196616 | tf_op jit(solution)/shard_map/ppermute | solution.py:23
  115.7 106.8 %copy-start.46 = (f32[8192]{0:T(1024)S(1)}, f32[8192]{0:T(1024)}, u32[]{:S(2)}) copy-start(f32[8192]{0:T(1024)} %param.17) | copy-start | bytes 98308
  232.4 1.4 copy-start.29
  235.2 35.8 %copy-start.1 = (bf16[1024,1024]{1,0:T(8,128)(2,1)S(1)}, bf16[1024,1024]{1,0:T(8,128)(2,1)}, u32[]{:S(2)}) copy-start(bf16[1024,1024]{1,0:T(8,128)(2,1)} %all-gather.7.cloned.1.call-done) | copy-start | bytes 6291460
  264.2 2.2 copy-start.21
  268.6 0.7 copy-start.19
  270.0 1.5 copy-start.7
  270.1 1.5 copy-start.12
  271.0 1.5 copy-start.42
  271.5 2.7 copy-start.3
  271.9 0.6 copy-start.25
  279.8 2.0 copy-start.27
  280.5 1.4 copy-start.39
  289.7 2.3 copy-start.22
  289.7 2.3 copy-start.37
  289.7 2.5 copy-start.40
  289.7 3.7 %copy-start.34 = (f32[1024]{0:T(1024)S(1)}, f32[1024]{0:T(1024)}, u32[]{:S(2)}) copy-start(f32[1024]{0:T(1024)} %param.21) | copy-start | bytes 12292
  292.7 0.7 copy-start.20
  293.5 1.5 copy-start.8
  293.6 1.5 copy-start.13
  294.5 1.5 copy-start.43
  295.0 2.1 copy-start.4
  295.4 0.6 copy-start.26
  302.7 1.4 copy-start.28
  311.3 2.2 copy-start.23
  315.7 0.7 copy-start.17
  317.2 1.5 copy-start.9
  317.2 1.5 copy-start.14
  318.2 0.9 copy-start.44
  318.7 1.2 copy-start.5
  318.8 1.6 copy-start.10
  318.8 1.6 copy-start.15
  319.1 2.0 copy-start.30
  320.2 1.9 copy-start.31
  321.0 2.5 copy-start.2
  321.0 2.5 copy-start.18
  322.1 2.0 copy-start.24
  322.1 2.0 copy-start.38
  (2 other events, 1.2 us)
Sparse Core Ops, SparseCore 0:
  9.5 40.9 all-gather.8
  52.6 41.8 all-gather.6
  96.7 125.7 all-gather.4
  224.5 39.6 all-gather.10
